TPU v7x, 32 devices: a whole 2x2x4 slice. The times are simulated.
32 devices in a mesh: theta: 16 (over z, x, core), gz: 2 (over y).
Axes of the slice: x: 2, y: 2, z: 4, core: 2. Of those that a mesh axis runs over, the one named last changes fastest.
Arguments:
- field: float32 [16, 1024, 1024], P('gz', 'theta'), parts along dimension 0, may hold values from -6 to 6
- courant: float32 [1024], replicated, may hold values from 0.2 to 0.8
Outputs:
- advanced: float32 [16, 1024, 1024], P('gz', 'theta'), parts along dimension 0
There are 2 independent parts, one for each index of `gz`. A program takes and returns all parts, laid end to end along the dimension named above; an argument that names none is the same for every part. Nothing has to cross between parts.
All inputs are finite; a program needn't handle non-finite values.
Results may differ from a plain program's by a relative error of at most 0.00007.
Values sent between devices are 32-bit elements; how exact they have to be, the bound alone decides.
A program may use at most 128 MiB of HBM per device.

v0:
```python
import functools

import jax
import jax.numpy as jnp
import numpy as np
from jax import lax
from jax.experimental import pallas as pl
from jax.experimental.pallas import tpu as pltpu
from jax.sharding import PartitionSpec as P

stencil_weights = (4.0 / 5.0, -1.0 / 5.0, 4.0 / 105.0, -1.0 / 280.0)
radial_step = 0.2
PLANES = 4
PAD = 8
TILE = 256
MESH = pl.DeviceIdType.MESH


def radial_tables(radial_count):
    last = 2 * radial_count - 1
    i = np.arange(radial_count)
    l = np.arange(last + 1)
    unit = np.pi / (2 * last)
    x = np.cos(2 * unit * i)
    high = x.astype(np.float32)
    low = (x - high.astype(np.float64)).astype(np.float32)
    gap = -2.0 * np.sin(unit * (i[:, None] + l)) * np.sin(unit * (i[:, None] - l))
    same = i[:, None] == l
    ci = np.where(i == 0, 2.0, 1.0)
    cl = np.where((l == 0) | (l == last), 2.0, 1.0)
    sign = np.where((i[:, None] + l) % 2 == 0, 1.0, -1.0)
    off = np.where(same, 0.0, ci[:, None] / cl * sign / np.where(same, 1.0, gap))
    diagonal = -off.sum(axis=1)
    mirror = off[i, last - i]
    scale = 0.5 * radial_step / last * np.sin(2 * unit * i) ** 2
    column = scale * ci * np.where(i % 2 == 0, 1.0, -1.0)
    row = np.where(i % 2 == 0, 1.0, -1.0) / ci
    even = scale * (diagonal + mirror)
    odd = scale * (diagonal - mirror)
    return np.stack([high, low, column, row, even, odd, 0 * x, 0 * x]).astype(np.float32)


def build_matrices(table, mats, radial_count):
    blk = 128

    @pl.loop(0, radial_count // blk)
    def _(lb):
        l0 = pl.multiple_of(lb * blk, blk)

        def down(k):
            return jnp.transpose(jnp.broadcast_to(table[k : k + 1, pl.ds(l0, blk)], (blk, blk)))

        high, low, row = down(0), down(1), down(3)
        rows = lax.broadcasted_iota(jnp.int32, (blk, blk), 0) + l0

        @pl.loop(0, radial_count // blk)
        def _(jb):
            j0 = pl.multiple_of(jb * blk, blk)
            cols = pl.ds(j0, blk)
            same = rows == lax.broadcasted_iota(jnp.int32, (blk, blk), 1) + j0
            near = (table[0:1, cols] - high) + (table[1:2, cols] - low)
            far = table[0:1, cols] + high
            near = 1.0 / jnp.where(same, 1.0, near)
            far = 1.0 / far
            factor = table[2:3, cols] * row
            even = jnp.where(same, table[4:5, cols], factor * (near - far))
            odd = jnp.where(same, table[5:6, cols], factor * (near + far))
            for k, m in enumerate((even, odd)):
                head = m.astype(jnp.bfloat16)
                mats[2 * k, pl.ds(l0, blk), cols] = head
                mats[2 * k + 1, pl.ds(l0, blk), cols] = (m - head.astype(jnp.float32)).astype(jnp.bfloat16)


def kernel(
    size,
    field,
    courant_in,
    table_in,
    out,
    courant,
    table,
    state,
    mats,
    split,
    deriv,
    edge_out,
    edge_in,
    table_sem,
    own_sem,
    in_send,
    in_recv,
    out_send,
    out_recv,
    edge_send,
    edge_recv,
):
    ring = size // PLANES
    heights, rows, radial_count = field.shape
    per = heights // PLANES
    half = PLANES // 2
    me = lax.axis_index("theta")
    g = lax.div(me, ring)
    q = lax.rem(me, ring)
    right = g * ring + lax.rem(q + 1, ring)
    left = g * ring + lax.rem(q + ring - 1, ring)
    high_bit, low_bit = lax.div(g, 2), lax.rem(g, 2)

    def partner(m):
        a, b = m // 2, m % 2
        return 2 * (high_bit + a - 2 * a * high_bit) + (low_bit + b - 2 * b * low_bit)

    order = (3, 2, 1)
    others = [partner(m) for m in order]
    body = pl.ds(PAD, rows)

    barrier = pltpu.get_barrier_semaphore()
    for d in [o * ring + q for o in others] + [right, left]:
        pl.semaphore_signal(barrier, inc=1, device_id={"theta": d}, device_id_type=MESH)
    pl.semaphore_wait(barrier, len(others) + 2)

    def incoming(h, k):
        o = others[k]
        return pltpu.make_async_remote_copy(
            field.at[o * per + h],
            state.at[0, h, g, body],
            in_send.at[h, k],
            in_recv.at[h, k],
            device_id={"theta": o * ring + q},
            device_id_type=MESH,
        )

    def outgoing(h, k):
        o = others[k]
        return pltpu.make_async_remote_copy(
            state.at[3, h, o, body],
            out.at[g * per + h],
            out_send.at[h, k],
            out_recv.at[h, k],
            device_id={"theta": o * ring + q},
            device_id_type=MESH,
        )

    def own_in(h):
        return pltpu.make_async_copy(field.at[g * per + h], state.at[0, h, g, body], own_sem.at[0, h])

    def own_out(h):
        return pltpu.make_async_copy(state.at[3, h, g, body], out.at[g * per + h], own_sem.at[1, h])

    def edge(sec, h, way):
        return pltpu.make_async_remote_copy(
            edge_out.at[sec, h, way],
            edge_in.at[sec, h, way],
            edge_send.at[sec, h, way],
            edge_recv.at[sec, h, way],
            device_id={"theta": right if way == 0 else left},
            device_id_type=MESH,
        )

    for h in range(per):
        for k in range(len(order)):
            incoming(h, k).start()
        own_in(h).start()

    loads = [
        pltpu.make_async_copy(table_in, table, table_sem.at[0]),
        pltpu.make_async_copy(courant_in, courant, table_sem.at[1]),
    ]
    for load in loads:
        load.start()
    for load in loads:
        load.wait()
    build_matrices(table, mats, radial_count)

    wrap_right = lax.div(q, ring - 1)
    wrap_left = lax.div(ring - 1 - q, ring - 1)
    pair_rows = half * rows
    tiles = radial_count // TILE

    @pl.loop(0, per * 3)
    def _(step):
        h = lax.div(step, 3)
        sec = lax.rem(step, 3)

        @pl.when(sec == 0)
        def _():
            own_in(h).wait()
            for k in range(len(order)):
                incoming(h, k).wait_recv()

        for s in range(PLANES):
            src = lax.rem(s + PLANES - wrap_right, PLANES)
            edge_out[sec, h, 0, 4 * s : 4 * s + 4] = state[sec, h, src, PAD + rows - 4 : PAD + rows]
            src = lax.rem(s + wrap_left, PLANES)
            edge_out[sec, h, 1, 4 * s : 4 * s + 4] = state[sec, h, src, PAD : PAD + 4]
        edge(sec, h, 0).start()
        edge(sec, h, 1).start()

        @pl.loop(0, tiles)
        def _(c):
            cols = pl.ds(pl.multiple_of(c * TILE, TILE), TILE)
            for s in range(half):
                a = state[sec, h, s, body, cols]
                b = state[sec, h, s + half, body, cols]
                for k, w in enumerate((a + b, a - b)):
                    head = w.astype(jnp.bfloat16)
                    tail = (w - head.astype(jnp.float32)).astype(jnp.bfloat16)
                    split[k, s * rows : (s + 1) * rows, cols] = head
                    split[k, pair_rows + s * rows : pair_rows + (s + 1) * rows, cols] = tail

        @pl.loop(0, tiles)
        def _(c):
            cols = pl.ds(pl.multiple_of(c * TILE, TILE), TILE)
            parts = []
            for k in range(2):
                both = jnp.dot(split[k], mats[2 * k, :, cols], preferred_element_type=jnp.float32)
                rest = jnp.dot(
                    split[k, :pair_rows], mats[2 * k + 1, :, cols], preferred_element_type=jnp.float32
                )
                parts.append(both[:pair_rows] + (both[pair_rows:] + rest))
            deriv[0, :, cols] = parts[0] + parts[1]
            deriv[1, :, cols] = parts[0] - parts[1]

        edge(sec, h, 0).wait()
        edge(sec, h, 1).wait()
        for s in range(PLANES):
            state[sec, h, s, PAD - 4 : PAD] = edge_in[sec, h, 0, 4 * s : 4 * s + 4]
            state[sec, h, s, PAD + rows : PAD + rows + 4] = edge_in[sec, h, 1, 4 * s : 4 * s + 4]

        start_part = jnp.where(sec == 0, 0.0, jnp.where(sec == 1, 0.75, 1.0 / 3.0)).astype(jnp.float32)
        step_part = jnp.where(sec == 0, 1.0, jnp.where(sec == 1, 0.25, 2.0 / 3.0)).astype(jnp.float32)

        @pl.loop(0, tiles)
        def _(c):
            cols = pl.ds(pl.multiple_of(c * TILE, TILE), TILE)
            speed = courant[:, cols]
            for s in range(PLANES):
                total = jnp.zeros((rows, TILE), jnp.float32)
                for o in range(1, 5):
                    total = total + stencil_weights[o - 1] * (
                        state[sec, h, s, PAD + o : PAD + o + rows, cols]
                        - state[sec, h, s, PAD - o : PAD - o + rows, cols]
                    )
                now = state[sec, h, s, body, cols]
                d = deriv[s // half, (s % half) * rows : (s % half + 1) * rows, cols]
                moved = now - speed * total - now * d
                state[sec + 1, h, s, body, cols] = start_part * state[0, h, s, body, cols] + step_part * moved

        @pl.when(sec == 2)
        def _():
            for k in (1, 2, 0):
                outgoing(h, k).start()
            own_out(h).start()

    for h in range(per):
        for k in range(len(order)):
            incoming(h, k).wait_send()
        own_out(h).wait()
    for h in range(per):
        for k in range(len(order)):
            outgoing(h, k).wait()


def body(size, field, courant):
    heights, rows, radial_count = field.shape
    per = heights // PLANES
    table = jnp.asarray(radial_tables(radial_count))
    f32, bf16 = jnp.float32, jnp.bfloat16
    dma = pltpu.SemaphoreType.DMA
    anywhere = pl.BlockSpec(memory_space=pl.ANY)
    return pl.pallas_call(
        functools.partial(kernel, size),
        out_shape=pltpu.VMEM(field.shape, f32),
        in_specs=[anywhere] * 3,
        out_specs=pl.BlockSpec(memory_space=pltpu.VMEM),
        scratch_shapes=[
            pltpu.VMEM((1, radial_count), f32),
            pltpu.VMEM(table.shape, f32),
            pltpu.VMEM((4, per, PLANES, rows + 2 * PAD, radial_count), f32),
            pltpu.VMEM((4, radial_count, radial_count), bf16),
            pltpu.VMEM((2, PLANES * rows, radial_count), bf16),
            pltpu.VMEM((2, PLANES // 2 * rows, radial_count), f32),
            pltpu.VMEM((3, per, 2, 4 * PLANES, radial_count), f32),
            pltpu.VMEM((3, per, 2, 4 * PLANES, radial_count), f32),
            dma((2,)),
            dma((2, per)),
            dma((per, PLANES - 1)),
            dma((per, PLANES - 1)),
            dma((per, PLANES - 1)),
            dma((per, PLANES - 1)),
            dma((3, per, 2)),
            dma((3, per, 2)),
        ],
        compiler_params=pltpu.CompilerParams(
            collective_id=0, has_side_effects=True, vmem_limit_bytes=40 << 20
        ),
    )(*[pltpu.with_memory_space_constraint(x, pltpu.HBM) for x in (field, courant.reshape(1, -1), table)])


def solution(mesh):
    size = mesh.shape["theta"]
    return jax.shard_map(
        functools.partial(body, size),
        mesh=mesh,
        in_specs=(P("gz", "theta", None), P()),
        out_specs=P("gz", "theta", None),
        check_vma=False,
    )
```

profile of v0, /device:TPU:8, one launch (start us, length us, event | category | flops | bytes accessed | tf_op | source)
XLA Modules:
  0.0 96.0 jit_solution(1161552554907662644)
XLA Ops:
  0.0 94.7 %shard_map.37 = f32[8,64,1024]{2,1,0:T(8,128)S(1)} custom-call(f32[8,64,1024]{2,1,0:T(8,128)} %field.1, f32[1,1024]{1,0:T(1,128)} %bitcast.1, f32[8,1024]{1,0:T(8,128)} %constant.2.clone.table_in), custom_call_target="tpu_custom_call" | custom-call | tf_op jit(solution)/shard_map/pallas_call | solution.py:270
  94.7 1.3 %copy.5 = f32[8,64,1024]{2,1,0:T(8,128)} copy(f32[8,64,1024]{2,1,0:T(8,128)S(1)} %shard_map.37) | data formatting | bytes 4194304
where the time goes:
time: 96.1 us; the launch traced here: 96 us
  Pallas kernels  94.7 us (99%)
  local copies, waits for them, and re-layouts  1.32 us (1%)
    pallas_call x1, Pallas kernels, body(): pl.pallas_call(functools.partial(kernel, size), out_shape=pltpu.VMEM(fiel...  94.7 us

commit v1 on v0

v1 whole, which is shorter than its diff:
```python
import functools
import math

import jax
import jax.numpy as jnp
import numpy as np
from jax import lax
from jax.experimental import pallas as pl
from jax.experimental.pallas import tpu as pltpu
from jax.sharding import PartitionSpec as P

stencil_weights = (4.0 / 5.0, -1.0 / 5.0, 4.0 / 105.0, -1.0 / 280.0)
radial_step = 0.2
BLOCK = 256
LANES = 128
FAR = 16
HALO = 4
GROUP = 8
MESH = pl.DeviceIdType.MESH
f32, bf16 = jnp.float32, jnp.bfloat16


def best_shifts(delta, count):
    a, g, c = [1.0], [delta], [math.sqrt(1.0 - delta * delta)]
    for _ in range(9):
        a.append((a[-1] + g[-1]) / 2)
        c.append((a[-2] - g[-1]) / 2)
        g.append(math.sqrt(a[-2] * g[-1]))
    quarter = math.pi / (2 * a[-1])
    shifts = []
    for i in range(count):
        phi = 2 ** (len(a) - 1) * a[-1] * (2 * i + 1) * quarter / (2 * count)
        for k in range(len(a) - 1, 0, -1):
            phi = 0.5 * (phi + math.asin(max(-1.0, min(1.0, c[k] / a[k] * math.sin(phi)))))
        shifts.append(math.sqrt(math.cos(phi) ** 2 + (delta * math.sin(phi)) ** 2))
    return shifts


def rational_terms(points, shifts):
    columns, product = [], np.ones_like(points)
    for p in shifts:
        columns.append(math.sqrt(2 * p) / (points + p) * product)
        product = product * (points - p) / (points + p)
    return np.stack(columns, axis=1)


def rank_for(delta, tolerance):
    return math.ceil(math.log(4 / tolerance) * math.log(4 / delta) / math.pi**2)


def split_head(m):
    head = m.astype(np.float32).astype(bf16)
    tail = (m - head.astype(np.float64)).astype(np.float32).astype(bf16)
    return head, tail


def radial_tables(radial_count):
    last = 2 * radial_count - 1
    i = np.arange(radial_count)
    l = np.arange(last + 1)
    unit = np.pi / (2 * last)
    x = np.cos(2 * unit * i)
    gap = -2.0 * np.sin(unit * (i[:, None] + l)) * np.sin(unit * (i[:, None] - l))
    same = i[:, None] == l
    ci = np.where(i == 0, 2.0, 1.0)
    cl = np.where((l == 0) | (l == last), 2.0, 1.0)
    sign = np.where((i[:, None] + l) % 2 == 0, 1.0, -1.0)
    off = np.where(same, 0.0, ci[:, None] / cl * sign / np.where(same, 1.0, gap))
    near = (off - np.where(same, off.sum(axis=1)[:, None], 0.0))[:, :radial_count].T
    scale = radial_step / last * np.sin(2 * unit * i) ** 2
    blocks = radial_count // BLOCK
    diag = np.stack(
        [(near * scale)[b * BLOCK : (b + 1) * BLOCK, b * BLOCK : (b + 1) * BLOCK] for b in range(blocks)]
    )
    alternate = np.where(i % 2 == 0, 1.0, -1.0)
    row, column = alternate / ci, alternate * ci * scale
    into = np.zeros((radial_count, LANES))
    back = np.zeros((LANES, radial_count))
    at = 0
    for b in range(blocks):
        first, final = b * BLOCK, (b + 1) * BLOCK - 1
        low, high = x[final], x[first]
        above = x[first - 1] if b > 0 else x[-1]
        below = x[final + 1] if b < blocks - 1 else x[0]
        ratio = -((high - above) * (below - low)) / ((high - low) * (below - above))
        delta = ratio / (ratio + 2 + 2 * math.sqrt(ratio + 1))
        turn = (delta - 1) / (delta + 1) * (high - below) / (high - low)
        under = (x - below) - turn * (x - low)
        mapped = ((x - below) + turn * (x - low)) / under
        det = 2 * turn * (low - below)
        inside = (i >= first) & (i <= final)
        count = rank_for(delta, 1e-10)
        shifts = best_shifts(delta, count)
        into[inside, at : at + count] = rational_terms(mapped[inside], shifts) / under[inside, None]
        outer = rational_terms(-mapped[~inside], shifts) / under[~inside, None]
        back[at : at + count, ~inside] = (-det * outer).T
        at += count
    assert at <= LANES - FAR
    far = rational_terms(x, best_shifts(x[-1], FAR))
    into[:, LANES - FAR :] = far
    back[LANES - FAR :] = -far.T
    into *= row[:, None]
    back *= column
    diag_parts = np.stack(split_head(diag))
    into_parts = np.concatenate(split_head(into), axis=1)
    back_head, back_tail = split_head(back)
    back_parts = np.stack(
        [np.concatenate([back_head, back_head]), np.concatenate([back_tail, back_tail])]
    )
    return diag_parts, into_parts, back_parts


def kernel(
    size,
    field,
    courant_in,
    diag_in,
    into_in,
    back_in,
    out,
    courant,
    diag,
    into,
    back,
    raw,
    state,
    head,
    tail,
    coef,
    pair,
    deriv,
    packed,
    inbox,
    load_sem,
    table_sem,
    halo_send,
    halo_recv,
    coef_send,
    coef_recv,
):
    heights, rows, radial_count = field.shape
    blocks = radial_count // BLOCK
    groups = rows // GROUP
    rest = groups - 1
    span = GROUP * heights
    inner = rest * span
    tiles = radial_count // LANES
    me = lax.axis_index("theta")
    right = lax.rem(me + 1, size)
    left = lax.rem(me + size - 1, size)
    across = lax.rem(me + size // 2, size)

    barrier = pltpu.get_barrier_semaphore()
    for d in (right, left, across):
        pl.semaphore_signal(barrier, inc=1, device_id={"theta": d}, device_id_type=MESH)

    loads = [
        pltpu.make_async_copy(
            field.at[h, :, pl.ds(t * LANES, LANES)], raw.at[t, pl.ds(h * rows, rows)], load_sem.at[t, h]
        )
        for t in range(tiles)
        for h in range(heights)
    ]
    pairs = ((courant_in, courant), (into_in, into), (diag_in, diag), (back_in, back))
    tables = [pltpu.make_async_copy(a, b, table_sem.at[k]) for k, (a, b) in enumerate(pairs)]
    for copy in loads + tables:
        copy.start()

    def halo(sec, way):
        if way == 0:
            source, target, device = HALO + rows - HALO, 0, right
        else:
            source, target, device = HALO, HALO + rows, left
        return pltpu.make_async_remote_copy(
            state.at[sec, pl.ds(source, HALO)],
            state.at[sec, pl.ds(target, HALO)],
            halo_send.at[sec, way],
            halo_recv.at[sec, way],
            device_id={"theta": device},
            device_id_type=MESH,
        )

    def coefs(sec, part):
        where = pl.ds(0, 1) if part == 0 else pl.ds(1, rest)
        return pltpu.make_async_remote_copy(
            packed.at[sec, where],
            inbox.at[sec, where],
            coef_send.at[sec, part],
            coef_recv.at[sec, part],
            device_id={"theta": across},
            device_id_type=MESH,
        )

    def keep_split(value, at, cols):
        value = value.reshape(-1, value.shape[-1])
        top = value.astype(bf16)
        head[pl.ds(at, value.shape[0]), cols] = top
        tail[pl.ds(at, value.shape[0]), cols] = (value - top.astype(f32)).astype(bf16)

    def place(g):
        return HALO + HALO + (g - 1) * GROUP

    lane = lax.broadcasted_iota(jnp.int32, (heights, LANES), 1)
    own = lane < LANES - FAR

    def project(at, count, sec, first_group, group_count):
        both = jnp.dot(head[pl.ds(at, count)], into[...], preferred_element_type=f32) + jnp.dot(
            tail[pl.ds(at, count)], into[...], preferred_element_type=f32
        )
        total = both[:, :LANES] + both[:, LANES:]
        coef[pl.ds(at, count)] = total
        for g in range(group_count):
            pack = jnp.zeros((heights, LANES), f32)
            for k in range(GROUP):
                r = g * span + k * heights
                moved = pltpu.roll(total[r : r + heights], (FAR * (k + 1)) % LANES, 1)
                pack = jnp.where((lane >= FAR * k) & (lane < FAR * (k + 1)), moved, pack)
            packed[sec, first_group + g] = pack

    def merge(sec, first_group, group_count):
        for g in range(first_group, first_group + group_count):
            pack = inbox[sec, g]
            mixed = []
            for k in range(GROUP):
                r = g * span + k * heights
                moved = pltpu.roll(pack, (LANES - FAR * (k + 1)) % LANES, 1)
                mixed.append(jnp.where(own, coef[r : r + heights], moved))
            mixed = jnp.concatenate(mixed, axis=0)
            top = mixed.astype(bf16)
            pair[pl.ds(g * span, span), 0:LANES] = top
            pair[pl.ds(g * span, span), LANES : 2 * LANES] = (mixed - top.astype(f32)).astype(bf16)

    def differentiate(at, count):
        where = pl.ds(at, count)

        @pl.loop(0, blocks)
        def _(b):
            cols = pl.ds(pl.multiple_of(b * BLOCK, BLOCK), BLOCK)
            top = head[where, cols]
            both = pair[where]
            deriv[where, cols] = (
                jnp.dot(top, diag[0, b], preferred_element_type=f32)
                + jnp.dot(tail[where, cols], diag[0, b], preferred_element_type=f32)
                + jnp.dot(top, diag[1, b], preferred_element_type=f32)
                + jnp.dot(both, back[0, :, cols], preferred_element_type=f32)
                + jnp.dot(both, back[1, :, cols], preferred_element_type=f32)
            )

    def update(sec, first, count, at):
        start_part = (0.0, 0.75, 1.0 / 3.0)[sec]
        step_part = (1.0, 0.25, 2.0 / 3.0)[sec]
        for t in range(tiles):
            cols = slice(t * LANES, (t + 1) * LANES)
            speed = jnp.broadcast_to(courant[:, cols], (heights, LANES))
            x = state[sec, pl.ds(first - HALO, count + 2 * HALO), :, cols]
            now = x[HALO : HALO + count]
            azimuth = None
            for o in range(1, 5):
                term = stencil_weights[o - 1] * (x[HALO + o : HALO + o + count] - x[HALO - o : HALO - o + count])
                azimuth = term if azimuth is None else azimuth + term
            slope = deriv[pl.ds(at, count * heights), cols].reshape(count, heights, LANES)
            moved = now - speed * azimuth - now * slope
            if sec > 0:
                moved = start_part * state[0, pl.ds(first, count), :, cols] + step_part * moved
            if sec < 2:
                state[sec + 1, pl.ds(first, count), :, cols] = moved
                keep_split(moved, at, cols)
            else:
                raw[t, pl.ds((first - HALO) * heights, count * heights)] = moved.reshape(-1, LANES)

    def emit(g):
        for t in range(tiles):
            for h in range(heights):
                out[pl.ds(pl.multiple_of(h * rows + g * GROUP, GROUP), GROUP), t * LANES : (t + 1) * LANES] = raw[
                    t, pl.ds(g * span + h, GROUP, stride=heights)
                ]

    for copy in loads:
        copy.wait()

    def stage(first, count, at):
        for t in range(tiles):
            cols = slice(t * LANES, (t + 1) * LANES)
            value = jnp.stack([raw[t, pl.ds(first - HALO + k, heights, stride=rows)] for k in range(count)])
            state[0, pl.ds(first, count), :, cols] = value
            keep_split(value, at, cols)

    stage(HALO, HALO, 0)
    stage(rows, HALO, HALO * heights)

    @pl.loop(1, groups)
    def _(g):
        stage(place(g), GROUP, pl.multiple_of(g * span, span))

    pl.semaphore_wait(barrier, 3)
    halo(0, 0).start()
    halo(0, 1).start()
    for copy in tables:
        copy.wait()
    project(0, span, 0, 0, 1)
    coefs(0, 0).start()
    project(span, inner, 0, 1, rest)
    coefs(0, 1).start()

    for sec in range(3):
        coefs(sec, 1).wait_recv()
        merge(sec, 1, rest)
        differentiate(span, inner)

        @pl.loop(1, groups)
        def _(g):
            update(sec, place(g), GROUP, pl.multiple_of(g * span, span))

        if sec < 2:
            project(span, inner, sec + 1, 1, rest)
            coefs(sec + 1, 1).start()
        else:

            @pl.loop(1, groups - 1)
            def _(g):
                emit(g)

        coefs(sec, 0).wait_recv()
        merge(sec, 0, 1)
        differentiate(0, span)
        halo(sec, 0).wait_recv()
        halo(sec, 1).wait_recv()
        update(sec, HALO, HALO, 0)
        update(sec, rows, HALO, HALO * heights)
        if sec < 2:
            halo(sec + 1, 0).start()
            halo(sec + 1, 1).start()
            project(0, span, sec + 1, 0, 1)
            coefs(sec + 1, 0).start()
    emit(0)
    emit(groups - 1)

    for sec in range(3):
        for k in range(2):
            halo(sec, k).wait_send()
            coefs(sec, k).wait_send()


def body(size, field, courant):
    heights, rows, radial_count = field.shape
    tables = [jnp.asarray(t) for t in radial_tables(radial_count)]
    groups = rows // GROUP
    dma = pltpu.SemaphoreType.DMA
    anywhere = pl.BlockSpec(memory_space=pl.ANY)
    operands = [field, courant.reshape(1, -1)] + tables
    result = pl.pallas_call(
        functools.partial(kernel, size),
        out_shape=pltpu.VMEM((heights * rows, radial_count), f32),
        in_specs=[anywhere] * len(operands),
        out_specs=pl.BlockSpec(memory_space=pltpu.VMEM),
        scratch_shapes=[
            pltpu.VMEM((1, radial_count), f32),
            *[pltpu.VMEM(t.shape, bf16) for t in tables],
            pltpu.VMEM((radial_count // LANES, heights * rows, LANES), f32),
            pltpu.VMEM((3, rows + 2 * HALO, heights, radial_count), f32),
            pltpu.VMEM((rows * heights, radial_count), bf16),
            pltpu.VMEM((rows * heights, radial_count), bf16),
            pltpu.VMEM((rows * heights, LANES), f32),
            pltpu.VMEM((rows * heights, 2 * LANES), bf16),
            pltpu.VMEM((rows * heights, radial_count), f32),
            pltpu.VMEM((3, groups, heights, LANES), f32),
            pltpu.VMEM((3, groups, heights, LANES), f32),
            dma((radial_count // LANES, heights)),
            dma((4,)),
            dma((3, 2)),
            dma((3, 2)),
            dma((3, 2)),
            dma((3, 2)),
        ],
        compiler_params=pltpu.CompilerParams(
            collective_id=0, has_side_effects=True, vmem_limit_bytes=40 << 20
        ),
    )(*[pltpu.with_memory_space_constraint(x, pltpu.HBM) for x in operands])
    return result.reshape(field.shape)


def solution(mesh):
    size = mesh.shape["theta"]
    return jax.shard_map(
        functools.partial(body, size),
        mesh=mesh,
        in_specs=(P("gz", "theta", None), P()),
        out_specs=P("gz", "theta", None),
        check_vma=False,
    )
```

time: 96.1 us -> 33.3 us (0.35)
  the two profiles are of different devices: /device:TPU:8 before, /device:TPU:0 now
where the time goes in v1:
time: 33.3 us; the launch traced here: 33.1 us
  Pallas kernels  31.8 us (95%)
  local copies, waits for them, and re-layouts  1.32 us (4%)
    pallas_call x1, Pallas kernels, body(): pl.pallas_call(functools.partial(kernel, size), out_shape=pltpu.VMEM((hei...  31.8 us
    unnamed x1, local copies, waits for them, and re-layouts  1.32 us

profile of v1, /device:TPU:0, one launch (start us, length us, event | category | flops | bytes accessed | tf_op | source)
XLA Modules:
  0.0 33.1 jit_solution(128712363860668301)
XLA Ops:
  0.0 31.8 %shard_map.55 = f32[512,1024]{1,0:T(8,128)S(1)} custom-call(f32[8,64,1024]{2,1,0:T(8,128)} %field.1, f32[1,1024]{1,0:T(1,128)} %bitcast.3, bf16[2,4,256,256]{3,2,1,0:T(8,128)(2,1)} %constant.6.clone.diag_in, bf16[1024,256]{1,0:T(8,128)(2,1)} %constant.7.clone.into_in, bf16[2,256,1024]{2,1,0:T(8,128)(2,1)} %constant.8.clone.back_in), custom_call_target="tpu_custom_call" | custom-call | tf_op jit(solution)/shard_map/pallas_call | solution.py:351
  31.8 1.3 %copy.7 = f32[8,64,1024]{2,1,0:T(8,128)} copy(f32[8,64,1024]{2,1,0:T(8,128)S(1)} %bitcast.2) | data formatting | bytes 4194304

commit v2 on v1

--- a/solution.py
+++ b/solution.py
@@ -18,6 +18,15 @@
 GROUP = 8
 MESH = pl.DeviceIdType.MESH
 f32, bf16 = jnp.float32, jnp.bfloat16
+fills = (
+    (0, 0, BLOCK),
+    (0, BLOCK, BLOCK),
+    (BLOCK, 2 * BLOCK, BLOCK),
+    (2 * BLOCK, 3 * BLOCK, LANES),
+    (2 * BLOCK, 3 * BLOCK + LANES, LANES),
+    (2 * BLOCK + LANES, 4 * BLOCK, LANES),
+    (2 * BLOCK + LANES, 4 * BLOCK + LANES, LANES),
+)
 
 
 def best_shifts(delta, count):
@@ -101,27 +110,24 @@
     back[LANES - FAR :] = -far.T
     into *= row[:, None]
     back *= column
-    diag_parts = np.stack(split_head(diag))
+    diag_head, diag_tail = split_head(diag)
     into_parts = np.concatenate(split_head(into), axis=1)
     back_head, back_tail = split_head(back)
-    back_parts = np.stack(
-        [np.concatenate([back_head, back_head]), np.concatenate([back_tail, back_tail])]
-    )
-    return diag_parts, into_parts, back_parts
+    back_head, back_tail = [m.reshape(LANES, blocks, BLOCK).transpose(1, 0, 2) for m in (back_head, back_tail)]
+    both_parts = np.concatenate([diag_head, diag_tail, back_head, back_tail], axis=1)
+    return into_parts, both_parts
 
 
 def kernel(
     size,
     field,
     courant_in,
-    diag_in,
     into_in,
-    back_in,
+    both_in,
     out,
     courant,
-    diag,
     into,
-    back,
+    both,
     raw,
     state,
     head,
@@ -141,9 +147,9 @@
     heights, rows, radial_count = field.shape
     blocks = radial_count // BLOCK
     groups = rows // GROUP
-    rest = groups - 1
     span = GROUP * heights
-    inner = rest * span
+    middle = (groups + 2) // 2
+    parts = ((0, 1), (1, middle), (middle, groups))
     tiles = radial_count // LANES
     me = lax.axis_index("theta")
     right = lax.rem(me + 1, size)
@@ -161,27 +167,31 @@
         for t in range(tiles)
         for h in range(heights)
     ]
-    pairs = ((courant_in, courant), (into_in, into), (diag_in, diag), (back_in, back))
+    pairs = [(courant_in, courant), (into_in, into)]
+    for source, target, count in fills:
+        pairs.append((both_in.at[:, pl.ds(source, count)], both.at[:, pl.ds(target, count)]))
     tables = [pltpu.make_async_copy(a, b, table_sem.at[k]) for k, (a, b) in enumerate(pairs)]
     for copy in loads + tables:
         copy.start()
 
-    def halo(sec, way):
+    def halo(sec, way, b):
         if way == 0:
             source, target, device = HALO + rows - HALO, 0, right
         else:
             source, target, device = HALO, HALO + rows, left
+        cols = pl.ds(b * BLOCK, BLOCK)
         return pltpu.make_async_remote_copy(
-            state.at[sec, pl.ds(source, HALO)],
-            state.at[sec, pl.ds(target, HALO)],
-            halo_send.at[sec, way],
-            halo_recv.at[sec, way],
+            state.at[sec, pl.ds(source, HALO), :, cols],
+            state.at[sec, pl.ds(target, HALO), :, cols],
+            halo_send.at[sec, way, b],
+            halo_recv.at[sec, way, b],
             device_id={"theta": device},
             device_id_type=MESH,
         )
 
     def coefs(sec, part):
-        where = pl.ds(0, 1) if part == 0 else pl.ds(1, rest)
+        first, stop = parts[part]
+        where = pl.ds(first, stop - first)
         return pltpu.make_async_remote_copy(
             packed.at[sec, where],
             inbox.at[sec, where],
@@ -203,22 +213,27 @@
     lane = lax.broadcasted_iota(jnp.int32, (heights, LANES), 1)
     own = lane < LANES - FAR
 
-    def project(at, count, sec, first_group, group_count):
-        both = jnp.dot(head[pl.ds(at, count)], into[...], preferred_element_type=f32) + jnp.dot(
-            tail[pl.ds(at, count)], into[...], preferred_element_type=f32
+    def project(sec, part):
+        first, stop = parts[part]
+        where = slice(first * span, stop * span)
+        double = jnp.dot(head[where], into[...], preferred_element_type=f32) + jnp.dot(
+            tail[where], into[...], preferred_element_type=f32
         )
-        total = both[:, :LANES] + both[:, LANES:]
-        coef[pl.ds(at, count)] = total
-        for g in range(group_count):
+        total = double[:, :LANES] + double[:, LANES:]
+        coef[where] = total
+        for g in range(first, stop):
             pack = jnp.zeros((heights, LANES), f32)
             for k in range(GROUP):
-                r = g * span + k * heights
+                r = (g - first) * span + k * heights
                 moved = pltpu.roll(total[r : r + heights], (FAR * (k + 1)) % LANES, 1)
                 pack = jnp.where((lane >= FAR * k) & (lane < FAR * (k + 1)), moved, pack)
-            packed[sec, first_group + g] = pack
-
-    def merge(sec, first_group, group_count):
-        for g in range(first_group, first_group + group_count):
+            packed[sec, g] = pack
+        coefs(sec, part).start()
+
+    def differentiate(sec, part):
+        first, stop = parts[part]
+        coefs(sec, part).wait_recv()
+        for g in range(first, stop):
             pack = inbox[sec, g]
             mixed = []
             for k in range(GROUP):
@@ -227,29 +242,20 @@
                 mixed.append(jnp.where(own, coef[r : r + heights], moved))
             mixed = jnp.concatenate(mixed, axis=0)
             top = mixed.astype(bf16)
-            pair[pl.ds(g * span, span), 0:LANES] = top
-            pair[pl.ds(g * span, span), LANES : 2 * LANES] = (mixed - top.astype(f32)).astype(bf16)
-
-    def differentiate(at, count):
-        where = pl.ds(at, count)
-
-        @pl.loop(0, blocks)
-        def _(b):
-            cols = pl.ds(pl.multiple_of(b * BLOCK, BLOCK), BLOCK)
+            pair[g * span : (g + 1) * span, 0:LANES] = top
+            pair[g * span : (g + 1) * span, LANES : 2 * LANES] = (mixed - top.astype(f32)).astype(bf16)
+        where = slice(first * span, stop * span)
+        for b in range(blocks):
+            cols = slice(b * BLOCK, (b + 1) * BLOCK)
             top = head[where, cols]
-            both = pair[where]
-            deriv[where, cols] = (
-                jnp.dot(top, diag[0, b], preferred_element_type=f32)
-                + jnp.dot(tail[where, cols], diag[0, b], preferred_element_type=f32)
-                + jnp.dot(top, diag[1, b], preferred_element_type=f32)
-                + jnp.dot(both, back[0, :, cols], preferred_element_type=f32)
-                + jnp.dot(both, back[1, :, cols], preferred_element_type=f32)
-            )
-
-    def update(sec, first, count, at):
+            far = pair[where]
+            wide = jnp.concatenate([top, tail[where, cols], top, far, far], axis=1)
+            deriv[where, cols] = jnp.dot(wide, both[b], preferred_element_type=f32)
+
+    def update(sec, first, count, at, b):
         start_part = (0.0, 0.75, 1.0 / 3.0)[sec]
         step_part = (1.0, 0.25, 2.0 / 3.0)[sec]
-        for t in range(tiles):
+        for t in range(b * BLOCK // LANES, (b + 1) * BLOCK // LANES):
             cols = slice(t * LANES, (t + 1) * LANES)
             speed = jnp.broadcast_to(courant[:, cols], (heights, LANES))
             x = state[sec, pl.ds(first - HALO, count + 2 * HALO), :, cols]
@@ -292,53 +298,57 @@
     def _(g):
         stage(place(g), GROUP, pl.multiple_of(g * span, span))
 
+    def inner(sec, part):
+        differentiate(sec, part)
+        for b in range(blocks):
+            for g in range(*parts[part]):
+                update(sec, place(g), GROUP, g * span, b)
+        if sec < 2:
+            project(sec + 1, part)
+
+    def edges(sec):
+        differentiate(sec, 0)
+        for b in range(blocks):
+            halo(sec, 0, b).wait_recv()
+            halo(sec, 1, b).wait_recv()
+            update(sec, HALO, HALO, 0, b)
+            update(sec, rows, HALO, HALO * heights, b)
+            if sec < 2:
+                halo(sec + 1, 0, b).start()
+                halo(sec + 1, 1, b).start()
+        if sec < 2:
+            project(sec + 1, 0)
+
     pl.semaphore_wait(barrier, 3)
-    halo(0, 0).start()
-    halo(0, 1).start()
+    for b in range(blocks):
+        halo(0, 0, b).start()
+        halo(0, 1, b).start()
     for copy in tables:
         copy.wait()
-    project(0, span, 0, 0, 1)
-    coefs(0, 0).start()
-    project(span, inner, 0, 1, rest)
-    coefs(0, 1).start()
-
-    for sec in range(3):
-        coefs(sec, 1).wait_recv()
-        merge(sec, 1, rest)
-        differentiate(span, inner)
-
-        @pl.loop(1, groups)
-        def _(g):
-            update(sec, place(g), GROUP, pl.multiple_of(g * span, span))
-
-        if sec < 2:
-            project(span, inner, sec + 1, 1, rest)
-            coefs(sec + 1, 1).start()
-        else:
-
-            @pl.loop(1, groups - 1)
-            def _(g):
-                emit(g)
-
-        coefs(sec, 0).wait_recv()
-        merge(sec, 0, 1)
-        differentiate(0, span)
-        halo(sec, 0).wait_recv()
-        halo(sec, 1).wait_recv()
-        update(sec, HALO, HALO, 0)
-        update(sec, rows, HALO, HALO * heights)
-        if sec < 2:
-            halo(sec + 1, 0).start()
-            halo(sec + 1, 1).start()
-            project(0, span, sec + 1, 0, 1)
-            coefs(sec + 1, 0).start()
+    for part in range(len(parts)):
+        project(0, part)
+
+    for sec in range(2):
+        inner(sec, 1)
+        edges(sec)
+        inner(sec, 2)
+    inner(2, 1)
+    inner(2, 2)
+
+    @pl.loop(1, groups - 1)
+    def _(g):
+        emit(g)
+
+    edges(2)
     emit(0)
     emit(groups - 1)
 
     for sec in range(3):
-        for k in range(2):
-            halo(sec, k).wait_send()
-            coefs(sec, k).wait_send()
+        for way in range(2):
+            for b in range(blocks):
+                halo(sec, way, b).wait_send()
+        for part in range(len(parts)):
+            coefs(sec, part).wait_send()
 
 
 def body(size, field, courant):
@@ -355,7 +365,8 @@
         out_specs=pl.BlockSpec(memory_space=pltpu.VMEM),
         scratch_shapes=[
             pltpu.VMEM((1, radial_count), f32),
-            *[pltpu.VMEM(t.shape, bf16) for t in tables],
+            pltpu.VMEM(tables[0].shape, bf16),
+            pltpu.VMEM((radial_count // BLOCK, 5 * BLOCK, BLOCK), bf16),
             pltpu.VMEM((radial_count // LANES, heights * rows, LANES), f32),
             pltpu.VMEM((3, rows + 2 * HALO, heights, radial_count), f32),
             pltpu.VMEM((rows * heights, radial_count), bf16),
@@ -366,11 +377,11 @@
             pltpu.VMEM((3, groups, heights, LANES), f32),
             pltpu.VMEM((3, groups, heights, LANES), f32),
             dma((radial_count // LANES, heights)),
-            dma((4,)),
-            dma((3, 2)),
-            dma((3, 2)),
-            dma((3, 2)),
-            dma((3, 2)),
+            dma((2 + len(fills),)),
+            dma((3, 2, radial_count // BLOCK)),
+            dma((3, 2, radial_count // BLOCK)),
+            dma((3, 3)),
+            dma((3, 3)),
         ],
         compiler_params=pltpu.CompilerParams(
             collective_id=0, has_side_effects=True, vmem_limit_bytes=40 << 20

time: 33.3 us -> 29.9 us (0.90)
  Pallas kernels: 31.8 us -> 28.4 us
    pallas_call x1, Pallas kernels: 31.8 us -> 28.4 us  [body(): pl.pallas_call(functools.partial(kernel, size), out_shape=pltpu.VMEM((hei...]
where the time goes in v2:
time: 29.9 us; the launch traced here: 29.8 us
  Pallas kernels  28.4 us (95%)
  local copies, waits for them, and re-layouts  1.32 us (4%)
    pallas_call x1, Pallas kernels, body(): pl.pallas_call(functools.partial(kernel, size), out_shape=pltpu.VMEM((hei...  28.4 us
    unnamed x1, local copies, waits for them, and re-layouts  1.32 us

profile of v2, /device:TPU:0, one launch (start us, length us, event | category | flops | bytes accessed | tf_op | source)
XLA Modules:
  0.0 29.8 jit_solution(5504083694581139782)
XLA Ops:
  0.0 28.4 %shard_map.46 = f32[512,1024]{1,0:T(8,128)S(1)} custom-call(f32[8,64,1024]{2,1,0:T(8,128)} %field.1, f32[1,1024]{1,0:T(1,128)} %bitcast.3, bf16[1024,256]{1,0:T(8,128)(2,1)} %constant.4.clone.into_in, bf16[4,768,256]{2,1,0:T(8,128)(2,1)} %constant.5.clone.both_in), custom_call_target="tpu_custom_call" | custom-call | tf_op jit(solution)/shard_map/pallas_call | solution.py:361
  28.4 1.3 %copy.6 = f32[8,64,1024]{2,1,0:T(8,128)} copy(f32[8,64,1024]{2,1,0:T(8,128)S(1)} %bitcast.2) | data formatting | bytes 4194304

commit v3 on v2

--- a/solution.py
+++ b/solution.py
@@ -228,7 +228,6 @@
                 moved = pltpu.roll(total[r : r + heights], (FAR * (k + 1)) % LANES, 1)
                 pack = jnp.where((lane >= FAR * k) & (lane < FAR * (k + 1)), moved, pack)
             packed[sec, g] = pack
-        coefs(sec, part).start()
 
     def differentiate(sec, part):
         first, stop = parts[part]
@@ -305,6 +304,7 @@
                 update(sec, place(g), GROUP, g * span, b)
         if sec < 2:
             project(sec + 1, part)
+            coefs(sec + 1, part).start()
 
     def edges(sec):
         differentiate(sec, 0)
@@ -318,20 +318,26 @@
                 halo(sec + 1, 1, b).start()
         if sec < 2:
             project(sec + 1, 0)
-
+            coefs(sec + 1, 0).start()
+
+    for copy in tables:
+        copy.wait()
+    for part in (1, 2, 0):
+        project(0, part)
     pl.semaphore_wait(barrier, 3)
+    for part in (1, 2, 0):
+        coefs(0, part).start()
     for b in range(blocks):
         halo(0, 0, b).start()
         halo(0, 1, b).start()
-    for copy in tables:
-        copy.wait()
-    for part in range(len(parts)):
-        project(0, part)
-
-    for sec in range(2):
-        inner(sec, 1)
-        edges(sec)
-        inner(sec, 2)
+
+    inner(0, 1)
+    inner(0, 2)
+    edges(0)
+    inner(1, 1)
+    inner(1, 2)
+    edges(1)
+
     inner(2, 1)
     inner(2, 2)
 

time: 29.9 us -> 28.3 us (0.946)
  Pallas kernels: 28.4 us -> 26.8 us
    pallas_call x1, Pallas kernels: 28.4 us -> 26.8 us  [body(): pl.pallas_call(functools.partial(kernel, size), out_shape=pltpu.VMEM((hei...]
where the time goes in v3:
time: 28.3 us; the launch traced here: 28.1 us
  Pallas kernels  26.8 us (95%)
  local copies, waits for them, and re-layouts  1.32 us (5%)
    pallas_call x1, Pallas kernels, body(): pl.pallas_call(functools.partial(kernel, size), out_shape=pltpu.VMEM((hei...  26.8 us
    unnamed x1, local copies, waits for them, and re-layouts  1.32 us

profile of v3, /device:TPU:0, one launch (start us, length us, event | category | flops | bytes accessed | tf_op | source)
XLA Modules:
  0.0 28.1 jit_solution(6689390700007438828)
XLA Ops:
  0.0 26.8 %shard_map.46 = f32[512,1024]{1,0:T(8,128)S(1)} custom-call(f32[8,64,1024]{2,1,0:T(8,128)} %field.1, f32[1,1024]{1,0:T(1,128)} %bitcast.3, bf16[1024,256]{1,0:T(8,128)(2,1)} %constant.4.clone.into_in, bf16[4,768,256]{2,1,0:T(8,128)(2,1)} %constant.5.clone.both_in), custom_call_target="tpu_custom_call" | custom-call | tf_op jit(solution)/shard_map/pallas_call | solution.py:367
  26.8 1.3 %copy.6 = f32[8,64,1024]{2,1,0:T(8,128)} copy(f32[8,64,1024]{2,1,0:T(8,128)S(1)} %bitcast.2) | data formatting | bytes 4194304

commit v4 on v3

--- a/solution.py
+++ b/solution.py
@@ -115,7 +115,10 @@
     back_head, back_tail = split_head(back)
     back_head, back_tail = [m.reshape(LANES, blocks, BLOCK).transpose(1, 0, 2) for m in (back_head, back_tail)]
     both_parts = np.concatenate([diag_head, diag_tail, back_head, back_tail], axis=1)
-    return into_parts, both_parts
+    head, tail = back_head[:, LANES - FAR :], back_tail[:, LANES - FAR :]
+    far_parts = np.concatenate([head, head, tail, tail], axis=1)
+    far_parts = np.concatenate([far_parts, np.zeros((blocks, LANES - 4 * FAR, BLOCK), far_parts.dtype)], axis=1)
+    return into_parts, both_parts, far_parts
 
 
 def kernel(
@@ -124,15 +127,17 @@
     courant_in,
     into_in,
     both_in,
+    across_in,
     out,
     courant,
     into,
     both,
+    across_back,
     raw,
     state,
     head,
     tail,
-    coef,
+    away,
     pair,
     deriv,
     packed,
@@ -167,7 +172,7 @@
         for t in range(tiles)
         for h in range(heights)
     ]
-    pairs = [(courant_in, courant), (into_in, into)]
+    pairs = [(courant_in, courant), (into_in, into), (across_in, across_back)]
     for source, target, count in fills:
         pairs.append((both_in.at[:, pl.ds(source, count)], both.at[:, pl.ds(target, count)]))
     tables = [pltpu.make_async_copy(a, b, table_sem.at[k]) for k, (a, b) in enumerate(pairs)]
@@ -211,7 +216,6 @@
         return HALO + HALO + (g - 1) * GROUP
 
     lane = lax.broadcasted_iota(jnp.int32, (heights, LANES), 1)
-    own = lane < LANES - FAR
 
     def project(sec, part):
         first, stop = parts[part]
@@ -220,7 +224,10 @@
             tail[where], into[...], preferred_element_type=f32
         )
         total = double[:, :LANES] + double[:, LANES:]
-        coef[where] = total
+        kept = jnp.where(lax.broadcasted_iota(jnp.int32, total.shape, 1) < LANES - FAR, total, 0.0)
+        top = kept.astype(bf16)
+        pair[where, 0:LANES] = top
+        pair[where, LANES : 2 * LANES] = (kept - top.astype(f32)).astype(bf16)
         for g in range(first, stop):
             pack = jnp.zeros((heights, LANES), f32)
             for k in range(GROUP):
@@ -229,27 +236,36 @@
                 pack = jnp.where((lane >= FAR * k) & (lane < FAR * (k + 1)), moved, pack)
             packed[sec, g] = pack
 
-    def differentiate(sec, part):
+    def near(part):
+        first, stop = parts[part]
+        where = slice(first * span, stop * span)
+        for b in range(blocks):
+            cols = slice(b * BLOCK, (b + 1) * BLOCK)
+            top = head[where, cols]
+            wide = jnp.concatenate([top, tail[where, cols], top, pair[where], pair[where]], axis=1)
+            deriv[where, cols] = jnp.dot(wide, both[b], preferred_element_type=f32)
+
+    def far(sec, part):
         first, stop = parts[part]
         coefs(sec, part).wait_recv()
         for g in range(first, stop):
             pack = inbox[sec, g]
-            mixed = []
+            top = pack.astype(bf16).astype(f32)
+            rest = pack - top
+            lines = []
             for k in range(GROUP):
-                r = g * span + k * heights
-                moved = pltpu.roll(pack, (LANES - FAR * (k + 1)) % LANES, 1)
-                mixed.append(jnp.where(own, coef[r : r + heights], moved))
-            mixed = jnp.concatenate(mixed, axis=0)
-            top = mixed.astype(bf16)
-            pair[g * span : (g + 1) * span, 0:LANES] = top
-            pair[g * span : (g + 1) * span, LANES : 2 * LANES] = (mixed - top.astype(f32)).astype(bf16)
+                line = jnp.zeros((heights, LANES), f32)
+                for n in range(4):
+                    moved = pltpu.roll(rest if n % 2 else top, (FAR * (n - k)) % LANES, 1)
+                    line = jnp.where((lane >= FAR * n) & (lane < FAR * (n + 1)), moved, line)
+                lines.append(line)
+            away[g * span : (g + 1) * span] = jnp.concatenate(lines, axis=0).astype(bf16)
         where = slice(first * span, stop * span)
         for b in range(blocks):
             cols = slice(b * BLOCK, (b + 1) * BLOCK)
-            top = head[where, cols]
-            far = pair[where]
-            wide = jnp.concatenate([top, tail[where, cols], top, far, far], axis=1)
-            deriv[where, cols] = jnp.dot(wide, both[b], preferred_element_type=f32)
+            deriv[where, cols] = deriv[where, cols] + jnp.dot(
+                away[where], across_back[b], preferred_element_type=f32
+            )
 
     def update(sec, first, count, at, b):
         start_part = (0.0, 0.75, 1.0 / 3.0)[sec]
@@ -298,7 +314,7 @@
         stage(place(g), GROUP, pl.multiple_of(g * span, span))
 
     def inner(sec, part):
-        differentiate(sec, part)
+        far(sec, part)
         for b in range(blocks):
             for g in range(*parts[part]):
                 update(sec, place(g), GROUP, g * span, b)
@@ -307,7 +323,7 @@
             coefs(sec + 1, part).start()
 
     def edges(sec):
-        differentiate(sec, 0)
+        far(sec, 0)
         for b in range(blocks):
             halo(sec, 0, b).wait_recv()
             halo(sec, 1, b).wait_recv()
@@ -331,13 +347,15 @@
         halo(0, 0, b).start()
         halo(0, 1, b).start()
 
-    inner(0, 1)
-    inner(0, 2)
-    edges(0)
-    inner(1, 1)
-    inner(1, 2)
-    edges(1)
-
+    for part in (1, 2, 0):
+        near(part)
+    for sec in range(2):
+        inner(sec, 1)
+        inner(sec, 2)
+        near(1)
+        edges(sec)
+        near(2)
+        near(0)
     inner(2, 1)
     inner(2, 2)
 
@@ -373,17 +391,18 @@
             pltpu.VMEM((1, radial_count), f32),
             pltpu.VMEM(tables[0].shape, bf16),
             pltpu.VMEM((radial_count // BLOCK, 5 * BLOCK, BLOCK), bf16),
+            pltpu.VMEM(tables[2].shape, bf16),
             pltpu.VMEM((radial_count // LANES, heights * rows, LANES), f32),
             pltpu.VMEM((3, rows + 2 * HALO, heights, radial_count), f32),
             pltpu.VMEM((rows * heights, radial_count), bf16),
             pltpu.VMEM((rows * heights, radial_count), bf16),
-            pltpu.VMEM((rows * heights, LANES), f32),
+            pltpu.VMEM((rows * heights, LANES), bf16),
             pltpu.VMEM((rows * heights, 2 * LANES), bf16),
             pltpu.VMEM((rows * heights, radial_count), f32),
             pltpu.VMEM((3, groups, heights, LANES), f32),
             pltpu.VMEM((3, groups, heights, LANES), f32),
             dma((radial_count // LANES, heights)),
-            dma((2 + len(fills),)),
+            dma((3 + len(fills),)),
             dma((3, 2, radial_count // BLOCK)),
             dma((3, 2, radial_count // BLOCK)),
             dma((3, 3)),

time: 28.3 us -> 27.6 us (0.975)
  the two profiles are of different devices: /device:TPU:0 before, /device:TPU:1 now
where the time goes in v4:
time: 27.6 us; the launch traced here: 27.4 us
  Pallas kernels  26.1 us (95%)
  local copies, waits for them, and re-layouts  1.32 us (5%)
    pallas_call x1, Pallas kernels, body(): pl.pallas_call(functools.partial(kernel, size), out_shape=pltpu.VMEM((hei...  26.1 us
    unnamed x1, local copies, waits for them, and re-layouts  1.32 us

profile of v4, /device:TPU:1, one launch (start us, length us, event | category | flops | bytes accessed | tf_op | source)
XLA Modules:
  0.0 27.4 jit_solution(358337529456737869)
XLA Ops:
  0.0 26.1 %shard_map.55 = f32[512,1024]{1,0:T(8,128)S(1)} custom-call(f32[8,64,1024]{2,1,0:T(8,128)} %field.1, f32[1,1024]{1,0:T(1,128)} %bitcast.3, bf16[1024,256]{1,0:T(8,128)(2,1)} %constant.6.clone.into_in, bf16[4,768,256]{2,1,0:T(8,128)(2,1)} %constant.7.clone.both_in, bf16[4,128,256]{2,1,0:T(8,128)(2,1)} %constant.8.clone.across_in), custom_call_target="tpu_custom_call" | custom-call | tf_op jit(solution)/shard_map/pallas_call | solution.py:385
  26.1 1.3 %copy.7 = f32[8,64,1024]{2,1,0:T(8,128)} copy(f32[8,64,1024]{2,1,0:T(8,128)S(1)} %bitcast.2) | data formatting | bytes 4194304

commit v5 on v4

--- a/solution.py
+++ b/solution.py
@@ -220,10 +220,15 @@
     def project(sec, part):
         first, stop = parts[part]
         where = slice(first * span, stop * span)
-        double = jnp.dot(head[where], into[...], preferred_element_type=f32) + jnp.dot(
-            tail[where], into[...], preferred_element_type=f32
+        for b in range(blocks):
+            cols = slice(b * BLOCK, (b + 1) * BLOCK)
+            line = jnp.concatenate([head[where, cols], tail[where, cols]], axis=1)
+            deriv[where, cols] = jnp.dot(
+                line, jnp.concatenate([into[cols], into[cols]], axis=0), preferred_element_type=f32
+            )
+        total = functools.reduce(
+            lambda a, b: a + b, [deriv[where, k * LANES : (k + 1) * LANES] for k in range(radial_count // LANES)]
         )
-        total = double[:, :LANES] + double[:, LANES:]
         kept = jnp.where(lax.broadcasted_iota(jnp.int32, total.shape, 1) < LANES - FAR, total, 0.0)
         top = kept.astype(bf16)
         pair[where, 0:LANES] = top

time: 27.6 us -> 26.8 us (0.971)
  the two profiles are of different devices: /device:TPU:1 before, /device:TPU:0 now
where the time goes in v5:
time: 26.8 us; the launch traced here: 26.5 us
  Pallas kernels  25.2 us (94%)
  local copies, waits for them, and re-layouts  1.32 us (5%)
    pallas_call x1, Pallas kernels, body(): pl.pallas_call(functools.partial(kernel, size), out_shape=pltpu.VMEM((hei...  25.2 us
    unnamed x1, local copies, waits for them, and re-layouts  1.32 us

profile of v5, /device:TPU:0, one launch (start us, length us, event | category | flops | bytes accessed | tf_op | source)
XLA Modules:
  0.0 26.5 jit_solution(17571371910166869218)
XLA Ops:
  0.0 25.2 %shard_map.55 = f32[512,1024]{1,0:T(8,128)S(1)} custom-call(f32[8,64,1024]{2,1,0:T(8,128)} %field.1, f32[1,1024]{1,0:T(1,128)} %bitcast.3, bf16[1024,256]{1,0:T(8,128)(2,1)} %constant.6.clone.into_in, bf16[4,768,256]{2,1,0:T(8,128)(2,1)} %constant.7.clone.both_in, bf16[4,128,256]{2,1,0:T(8,128)(2,1)} %constant.8.clone.across_in), custom_call_target="tpu_custom_call" | custom-call | tf_op jit(solution)/shard_map/pallas_call | solution.py:390
  25.2 1.3 %copy.7 = f32[8,64,1024]{2,1,0:T(8,128)} copy(f32[8,64,1024]{2,1,0:T(8,128)S(1)} %bitcast.2) | data formatting | bytes 4194304

commit v6 on v5

--- a/solution.py
+++ b/solution.py
@@ -153,7 +153,7 @@
     blocks = radial_count // BLOCK
     groups = rows // GROUP
     span = GROUP * heights
-    middle = (groups + 2) // 2
+    middle = groups // 2
     parts = ((0, 1), (1, middle), (middle, groups))
     tiles = radial_count // LANES
     me = lax.axis_index("theta")
@@ -172,7 +172,7 @@
         for t in range(tiles)
         for h in range(heights)
     ]
-    pairs = [(courant_in, courant), (into_in, into), (across_in, across_back)]
+    pairs = [(into_in, into), (courant_in, courant), (across_in, across_back)]
     for source, target, count in fills:
         pairs.append((both_in.at[:, pl.ds(source, count)], both.at[:, pl.ds(target, count)]))
     tables = [pltpu.make_async_copy(a, b, table_sem.at[k]) for k, (a, b) in enumerate(pairs)]
@@ -341,8 +341,7 @@
             project(sec + 1, 0)
             coefs(sec + 1, 0).start()
 
-    for copy in tables:
-        copy.wait()
+    tables[0].wait()
     for part in (1, 2, 0):
         project(0, part)
     pl.semaphore_wait(barrier, 3)
@@ -352,13 +351,15 @@
         halo(0, 0, b).start()
         halo(0, 1, b).start()
 
+    for copy in tables[1:]:
+        copy.wait()
     for part in (1, 2, 0):
         near(part)
     for sec in range(2):
         inner(sec, 1)
         inner(sec, 2)
+        edges(sec)
         near(1)
-        edges(sec)
         near(2)
         near(0)
     inner(2, 1)

time: 26.8 us -> 26.2 us (0.978)
  Pallas kernels: 25.2 us -> 24.4 us
    pallas_call x1, Pallas kernels: 25.2 us -> 24.4 us  [body(): pl.pallas_call(functools.partial(kernel, size), out_shape=pltpu.VMEM((hei...]
where the time goes in v6:
time: 26.2 us; the launch traced here: 25.7 us
  Pallas kernels  24.4 us (93%)
  local copies, waits for them, and re-layouts  1.32 us (5%)
    pallas_call x1, Pallas kernels, body(): pl.pallas_call(functools.partial(kernel, size), out_shape=pltpu.VMEM((hei...  24.4 us
    unnamed x1, local copies, waits for them, and re-layouts  1.32 us

profile of v6, /device:TPU:0, one launch (start us, length us, event | category | flops | bytes accessed | tf_op | source)
XLA Modules:
  0.0 25.7 jit_solution(13286204991067202982)
XLA Ops:
  0.0 24.4 %shard_map.55 = f32[512,1024]{1,0:T(8,128)S(1)} custom-call(f32[8,64,1024]{2,1,0:T(8,128)} %field.1, f32[1,1024]{1,0:T(1,128)} %bitcast.3, bf16[1024,256]{1,0:T(8,128)(2,1)} %constant.6.clone.into_in, bf16[4,768,256]{2,1,0:T(8,128)(2,1)} %constant.7.clone.both_in, bf16[4,128,256]{2,1,0:T(8,128)(2,1)} %constant.8.clone.across_in), custom_call_target="tpu_custom_call" | custom-call | tf_op jit(solution)/shard_map/pallas_call | solution.py:391
  24.4 1.3 %copy.7 = f32[8,64,1024]{2,1,0:T(8,128)} copy(f32[8,64,1024]{2,1,0:T(8,128)S(1)} %bitcast.2) | data formatting | bytes 4194304
